TPU v7x, 32 devices: a whole 2x2x4 slice. The times are simulated.
32 devices in a mesh: lm: 8 (over z, x), kf: 4 (over y, core).
Axes of the slice: x: 2, y: 2, z: 4, core: 2. Of those that a mesh axis runs over, the one named last changes fastest.
Arguments:
- residual_rows: bfloat16 [4096, 128], P(('lm', 'kf')), may hold values from -6 to 6
- jacobian: bfloat16 [4096, 15, 128], P(('lm', 'kf')), may hold values from -1.5 to 1.5
- nullspace: bfloat16 [4096, 128, 128], P(('lm', 'kf')), may hold values from -0.5 to 0.5
- frame_ids: int32 [4096, 64], P(('lm', 'kf')), may hold values from 0 to 16383, as said below
- obs_count: int32 [4096], P(('lm', 'kf')), may hold values from 4 to 64
- damping: float32 [15, 16384], P(None, 'kf'), may hold values from 1 to 10
- jacobi_scale: float32 [15, 16384], P(None, 'kf'), may hold values from 0.02 to 0.3
Outputs:
- solution: float32 [15, 16384], P(None, 'kf')
- residual: float32 [15, 16384], P(None, 'kf')
Inputs may be any that keep to these rules, and one draw needn't show every extreme that they name: `frame_ids`: within a block the keyframe ids rise strictly from slot to slot by 1 to 8. A block stored on the device with kf index w names only keyframes from 4096 * w up to but not including 4096 * (w + 2), and never one of 16384 or more.
All inputs are finite; a program needn't handle non-finite values.
Results may differ from a plain program's by a relative error of at most 0.005.
Values sent between devices are 32-bit elements; how exact they have to be, the bound alone decides.
A program may use at most 64 MiB of HBM per device.

v0:
```python
import jax
import jax.numpy as jnp
from jax import lax
from jax.sharding import PartitionSpec as P

ITERS = 2


def passed_along(array, axis, by):
    length = lax.axis_size(axis)
    pairs = [(i, i + by) for i in range(length) if 0 <= i + by < length]
    return lax.ppermute(array, axis, pairs)


def row_layout(frame_ids, obs_count, first_frame):
    slots = lax.broadcasted_iota(jnp.int32, frame_ids.shape, 1)
    live = (slots < obs_count[:, None]).astype(jnp.float32)
    return (jnp.repeat(frame_ids - first_frame, 2, axis=1), jnp.repeat(live, 2, axis=1))


def project(lifted, nullspace, live):
    lifted_half = (lifted * live).astype(jnp.bfloat16)
    inner = jnp.einsum(
        "brk,br->bk", nullspace, lifted_half, preferred_element_type=jnp.float32
    ).astype(jnp.bfloat16)
    spread = jnp.einsum("brk,bk->br", nullspace, inner, preferred_element_type=jnp.float32)
    return spread * live


def spread_back(spread, jacobian, row_ids, width):
    terms = jacobian * spread[:, None, :]
    terms = jnp.moveaxis(terms, 1, 0).reshape(jacobian.shape[1], -1)
    return jnp.zeros((jacobian.shape[1], width), jnp.float32).at[:, row_ids.reshape(-1)].add(terms)


def window_pair(field):
    return jnp.concatenate([field, passed_along(field, "kf", -1)], axis=1)


def fold_next(partial_value, frames):
    return partial_value[:, :frames] + passed_along(partial_value[:, frames:], "kf", 1)


def inner_window(left, right):
    return lax.psum(jnp.sum(left * right), "kf")


def shards(residual_rows, jacobian, nullspace, frame_ids, obs_count, damping, jacobi_scale):
    frames = damping.shape[1]
    row_ids, live = row_layout(frame_ids, obs_count, lax.axis_index("kf") * frames)

    def local_terms(window_field):
        if window_field is None:
            lifted = residual_rows.astype(jnp.float32)
        else:
            gathered = jnp.take(window_field, row_ids, axis=1)
            lifted = jnp.sum(jacobian * jnp.moveaxis(gathered, 0, 1), axis=1)
        return spread_back(project(lifted, nullspace, live), jacobian, row_ids, 2 * frames)

    def combine(partial_value):
        return lax.psum(fold_next(partial_value, frames), "lm")

    damp_part, scale_part = (damping, jacobi_scale)
    gradient = -combine(local_terms(None))
    residual = gradient
    solution = jnp.zeros_like(gradient)
    scaled = scale_part * residual
    direction = scaled
    energy = inner_window(residual, scaled)
    for step_index in range(ITERS):
        applied = combine(local_terms(window_pair(direction))) + damp_part * direction
        step_size = energy / inner_window(direction, applied)
        solution = solution + step_size * direction
        residual = residual - step_size * applied
        if step_index + 1 < ITERS:
            scaled = scale_part * residual
            fresh = inner_window(residual, scaled)
            direction = scaled + fresh / energy * direction
            energy = fresh
    return (solution, residual)


def solution(mesh):
    placed = (
        P(("lm", "kf"), None),
        P(("lm", "kf"), None, None),
        P(("lm", "kf"), None, None),
        P(("lm", "kf"), None),
        P(("lm", "kf")),
        P(None, "kf"),
        P(None, "kf"),
    )
    return jax.shard_map(
        shards,
        mesh=mesh,
        in_specs=placed,
        out_specs=(P(None, "kf"), P(None, "kf")),
        check_vma=False,
    )
```

profile of v0, /device:TPU:0, one launch (start us, length us, event | category | flops | bytes accessed | tf_op | source)
XLA Modules:
  0.0 765.3 jit_solution(5595085198218443961)
XLA Ops:
  9.0 3.5 fusion.28
  15.1 4.3 broadcast_in_dim.13.clone
  19.4 5.5 reshape_reshape.2
  25.1 4.7 copy.161
  29.8 89.9 %scatter_custom_fusion = f32[15,8192]{0,1:T(8,128)} fusion(s32[16384]{0:T(1024)S(1)} %bitcast.77, f32[16384,15]{1,0:T(8,128)} %bitcast.65, f32[]{:T(128)} %constant.1.clone.1), kind=kCustom, calls=%fused_computation.9 | custom fusion | flops 245760 | bytes 492032 | tf_op jit(solution)/shard_map/scatter-add | solution.py:33
  119.6 3.8 fusion.27
  123.5 3.0 copy.130
  126.4 3.1 collective-permute-start
  132.5 77.6 %all-reduce.5.cloned.1.call-done = f32[15,4096]{1,0:T(8,128)} async-done(((f32[15,4096]{1,0:T(8,128)}), f32[15,4096]{1,0:T(8,128)}) %all-reduce.5.cloned.1.call-update) | async-done | bytes 245776 | tf_op jit(solution)/shard_map/psum | solution.py:61
  214.5 2.7 copy.133
  217.2 56.6 %gather_fusion = f32[16384,15]{1,0:T(8,128)} fusion(f32[15,8192]{0,1:T(8,128)} %copy.133, s32[16384]{0:T(1024)S(1)} %bitcast_clamp_fusion), kind=kCustom, calls=%fused_computation.clone | custom fusion | bytes 2031616 | tf_op jit(solution)/shard_map/jit(_take)/gather | solution.py:56
  273.8 5.3 copy.134
  279.3 3.5 fusion.17
  285.4 4.7 copy.162
  290.1 89.9 %scatter_custom_fusion.1 = f32[15,8192]{0,1:T(8,128)} fusion(s32[16384]{0:T(1024)S(1)} %bitcast.78, f32[16384,15]{1,0:T(8,128)} %bitcast.66, f32[]{:T(128)} %constant.1.clone.1), kind=kCustom, calls=%fused_computation.7 | custom fusion | flops 245760 | bytes 492032 | tf_op jit(solution)/shard_map/scatter-add | solution.py:33
  380.0 3.8 fusion.26
  383.8 3.0 copy.139
  386.8 6.7 collective-permute-start.2
  396.7 72.9 %all-reduce.7.cloned.1.call-done = f32[15,4096]{1,0:T(8,128)} async-done(((f32[15,4096]{1,0:T(8,128)}), f32[15,4096]{1,0:T(8,128)}) %all-reduce.7.cloned.1.call-update) | async-done | bytes 245776 | tf_op jit(solution)/shard_map/psum | solution.py:61
  471.2 6.3 all-reduce
  481.3 7.2 psum.53
  493.3 2.7 copy.142
  496.0 56.6 %gather_fusion.1 = f32[16384,15]{1,0:T(8,128)} fusion(f32[15,8192]{0,1:T(8,128)} %copy.142, s32[16384]{0:T(1024)S(1)} %bitcast_clamp_fusion), kind=kCustom, calls=%fused_computation.1.clone | custom fusion | bytes 2031616 | tf_op jit(solution)/shard_map/jit(_take)/gather | solution.py:56
  552.6 5.4 copy.143
  558.1 3.5 fusion.13
  564.3 4.7 copy.163
  569.0 89.9 %scatter_custom_fusion.2 = f32[15,8192]{0,1:T(8,128)} fusion(s32[16384]{0:T(1024)} %bitcast.79, f32[16384,15]{1,0:T(8,128)} %bitcast.64, f32[]{:T(128)} %constant.1.clone.1), kind=kCustom, calls=%fused_computation.5 | custom fusion | flops 245760 | bytes 492032 | tf_op jit(solution)/shard_map/scatter-add | solution.py:33
  658.8 3.8 fusion.25
  662.7 3.0 copy.148
  665.6 6.1 collective-permute-start.4
  674.9 72.9 %all-reduce.9.cloned.1.call-done = f32[15,4096]{1,0:T(8,128)} async-done(((f32[15,4096]{1,0:T(8,128)}), f32[15,4096]{1,0:T(8,128)}) %all-reduce.9.cloned.1.call-update) | async-done | bytes 245776 | tf_op jit(solution)/shard_map/psum | solution.py:61
  749.4 6.3 psum.55
  (88 shorter events, 34.6 us)
Async XLA Ops:
  7.2 202.9 %all-reduce.5.cloned.1.call-start = ((), (), s32[]{:S(2)}) async-start(), calls=%async_computation | async-start | bytes 524288 | tf_op jit(solution)/shard_map/psum | solution.py:61
  8.9 3.6 copy-start
  8.9 6.0 copy-start.11
  15.1 9.9 %copy-start.3 = (bf16[128,15,128]{2,0,1:T(8,128)(2,1)S(1)}, bf16[128,15,128]{2,0,1:T(8,128)(2,1)}, u32[]{:S(2)}) copy-start(bf16[128,15,128]{2,0,1:T(8,128)(2,1)} %param.10) | copy-start | bytes 1474564
  25.0 265.1 %copy-start.10 = (s32[16384,1]{0,1:T(1,128)}, s32[16384,1]{0,1:T(1,128)S(1)}, u32[]{:S(2)}) copy-start(s32[16384,1]{0,1:T(1,128)S(1)} %compare_select_fusion) | copy-start | bytes 196612
  123.5 86.6 %copy-start.6 = (f32[15,4096]{1,0:T(8,128)S(1)}, f32[15,4096]{1,0:T(8,128)}, u32[]{:S(2)}) copy-start(f32[15,4096]{1,0:T(8,128)} %param.15) | copy-start | bytes 737284
  126.4 3.9 collective-permute-start
  132.0 337.5 %all-reduce.7.cloned.1.call-start = ((), (), s32[]{:S(2)}) async-start(), calls=%async_computation.1 | async-start | bytes 524288 | tf_op jit(solution)/shard_map/psum | solution.py:61
  132.2 147.0 %copy-start.8 = (f32[128,128]{1,0:T(8,128)}, f32[128,128]{1,0:T(8,128)S(1)}, u32[]{:S(2)}) copy-start(f32[128,128]{1,0:T(8,128)S(1)} %copy.135) | copy-start | bytes 196612
  211.0 3.4 collective-permute-start.1
  279.1 3.7 copy-start.1
  383.8 85.7 %copy-start.4 = (f32[15,4096]{1,0:T(8,128)S(1)}, f32[15,4096]{1,0:T(8,128)}, u32[]{:S(2)}) copy-start(f32[15,4096]{1,0:T(8,128)} %param.14) | copy-start | bytes 737284
  383.8 85.7 %copy-start.5 = (f32[15,4096]{1,0:T(8,128)S(1)}, f32[15,4096]{1,0:T(8,128)}, u32[]{:S(2)}) copy-start(f32[15,4096]{1,0:T(8,128)} %all-reduce.5.cloned.1.call-done) | copy-start | bytes 737284
  386.8 8.0 %collective-permute-start.2 = (f32[15,4096]{1,0:T(8,128)}, f32[15,4096]{1,0:T(8,128)}, u32[]{:S(2)}, u32[]{:S(2)}) collective-permute-start(f32[15,4096]{1,0:T(8,128)} %copy.139), channel_id=1, source_target_pairs={{0,1},{1,2},{2,3},{4,5},{5,6},{6,7},{8,9},{9,10},{10,11},{12,13},{... | collective-permute-start | bytes 737288 | tf_op jit(solution)/shard_map/ppermute | solution.py:12
  396.6 351.2 %all-reduce.9.cloned.1.call-start = ((), (), s32[]{:S(2)}) async-start(), calls=%async_computation.2 | async-start | bytes 524288 | tf_op jit(solution)/shard_map/psum | solution.py:61
  489.8 3.4 collective-permute-start.3
  552.6 5.5 copy-start.9
  557.9 3.7 copy-start.2
  662.7 94.3 %copy-start.7 = (f32[15,4096]{1,0:T(8,128)S(1)}, f32[15,4096]{1,0:T(8,128)}, u32[]{:S(2)}) copy-start(f32[15,4096]{1,0:T(8,128)} %get-tuple-element.19) | copy-start | bytes 737284
  665.6 7.5 collective-permute-start.4
Sparse Core Ops, SparseCore 0:
  132.2 77.8 all-reduce.4
  396.7 72.7 all-reduce.6
  675.0 72.7 all-reduce.8
where the time goes:
time: 766 us; the launch traced here: 765 us
  other arithmetic  285 us (37%)
  waiting for transfers between devices  227 us (30%)
  local copies, waits for them, and re-layouts  179 us (23%)
  blocking collectives  19.8 us (3%)
  starting transfers between devices  19 us (2%)
  between operations  18.1 us (2%)
  matrix products  17.3 us (2%)
    scatter-add x3, other arithmetic, spread_back(): jnp.zeros((jacobian.shape[1], width), jnp.float32)  270 us
    psum x3, waiting for transfers between devices, combine(): return lax.psum(fold_next(partial_value, frames), 'lm')  223 us
    gather x4, local copies, waits for them, and re-layouts, local_terms(): gathered = jnp.take(window_field, row_ids, axis=1)  124 us
    slice x6, local copies, waits for them, and re-layouts, fold_next(): partial_value[:, frames:]  20.4 us
    psum x3, blocking collectives, inner_window(): return lax.psum(jnp.sum(left * right), 'kf')  19.8 us
    ppermute x5, starting transfers between devices, passed_along(): return lax.ppermute(array, axis, pairs)  18.9 us
  transfers between devices with their start and end apart: 8, of which 6 were waited for; matrix products, arithmetic and copies ran while one was open for 0% of the time, Pallas kernels for 0%

commit v1 on v0

--- a/solution.py
+++ b/solution.py
@@ -58,7 +58,8 @@
         return spread_back(project(lifted, nullspace, live), jacobian, row_ids, 2 * frames)
 
     def combine(partial_value):
-        return lax.psum(fold_next(partial_value, frames), "lm")
+        fix_ways_now = lambda x_local: jnp.sum(lax.all_gather(x_local, "lm"), axis=0)
+        return fix_ways_now(fold_next(partial_value, frames))
 
     damp_part, scale_part = (damping, jacobi_scale)
     gradient = -combine(local_terms(None))

time: 766 us -> 702 us (0.916)
  waiting for transfers between devices: 227 us -> 164 us
    psum x3 -> x0, waiting for transfers between devices: 223 us -> none  [combine(): return lax.psum(fold_next(partial_value, frames), 'lm')]
    all_gather x0 -> x3, waiting for transfers between devices: none -> 157 us  [combine(): lax.all_gather(x_local, 'lm')]
    slice x6 -> x9, local copies, waits for them, and re-layouts: 20.4 us -> 6.63 us  [fold_next(): partial_value[:, frames:]]
    unnamed x0 -> x3, other arithmetic: none -> 9.51 us
  transfers between devices with their start and end apart: 8 -> 8, of which waited for: 6 -> 8; matrix products, arithmetic and copies ran while one was open for 0% -> 0% of each run, Pallas kernels for 0% -> 0%
where the time goes in v1:
time: 702 us; the launch traced here: 701 us
  other arithmetic  289 us (41%)
  local copies, waits for them, and re-layouts  174 us (25%)
  waiting for transfers between devices  164 us (23%)
  blocking collectives  19.8 us (3%)
  starting transfers between devices  18.4 us (3%)
  between operations  18.3 us (3%)
  matrix products  17.3 us (2%)
    scatter-add x3, other arithmetic, spread_back(): jnp.zeros((jacobian.shape[1], width), jnp.float32)  270 us
    all_gather x3, waiting for transfers between devices, combine(): lax.all_gather(x_local, 'lm')  157 us
    gather x4, local copies, waits for them, and re-layouts, local_terms(): gathered = jnp.take(window_field, row_ids, axis=1)  124 us
    psum x3, blocking collectives, inner_window(): return lax.psum(jnp.sum(left * right), 'kf')  19.8 us
    ppermute x5, starting transfers between devices, passed_along(): return lax.ppermute(array, axis, pairs)  18.3 us
    reshape x3, local copies, waits for them, and re-layouts, spread_back(): terms = jnp.moveaxis(terms, 1, 0).reshape(jacobian.shape[1], -1)  14.1 us
  transfers between devices with their start and end apart: 8, of which 8 were waited for; matrix products, arithmetic and copies ran while one was open for 0% of the time, Pallas kernels for 0%

profile of v1, /device:TPU:0, one launch (start us, length us, event | category | flops | bytes accessed | tf_op | source)
XLA Modules:
  0.0 701.4 jit_solution(12129009553198834177)
XLA Ops:
  9.0 3.5 fusion.28
  15.1 4.3 broadcast_in_dim.13.clone
  19.4 5.5 reshape_reshape.2
  25.1 4.7 copy.98
  29.8 89.9 %scatter_custom_fusion = f32[15,8192]{0,1:T(8,128)} fusion(s32[16384]{0:T(1024)S(1)} %bitcast.83, f32[16384,15]{1,0:T(8,128)} %bitcast.71, f32[]{:T(128)} %constant.1.clone.1), kind=kCustom, calls=%fused_computation.15 | custom fusion | flops 245760 | bytes 492032 | tf_op jit(solution)/shard_map/scatter-add | solution.py:33
  121.9 2.4 collective-permute-start
  126.1 3.2 fusion.2
  129.2 3.0 copy.65
  132.7 55.7 %all-gather.10.cloned.1.call-done = f32[8,15,4096]{2,1,0:T(8,128)} async-done(((f32[1,15,4096]{2,1,0:T(8,128)}), f32[8,15,4096]{2,1,0:T(8,128)}) %all-gather.10.cloned.1.call-update) | async-done | bytes 1966096 | tf_op jit(solution)/shard_map/all_gather | solution.py:61
  193.6 2.7 copy.68
  196.2 56.6 %gather_fusion = f32[16384,15]{1,0:T(8,128)} fusion(f32[15,8192]{0,1:T(8,128)} %copy.68, s32[16384]{0:T(1024)S(1)} %bitcast_clamp_fusion), kind=kCustom, calls=%fused_computation.clone | custom fusion | bytes 2031616 | tf_op jit(solution)/shard_map/jit(_take)/gather | solution.py:56
  252.8 5.3 copy.69
  258.4 3.5 fusion.20
  264.5 4.7 copy.99
  269.2 89.9 %scatter_custom_fusion.1 = f32[15,8192]{0,1:T(8,128)} fusion(s32[16384]{0:T(1024)} %bitcast.84, f32[16384,15]{1,0:T(8,128)} %bitcast.72, f32[]{:T(128)} %constant.1.clone.1), kind=kCustom, calls=%fused_computation.13 | custom fusion | flops 245760 | bytes 492032 | tf_op jit(solution)/shard_map/scatter-add | solution.py:33
  361.3 6.7 collective-permute-start.2
  370.1 3.2 fusion.1
  373.3 3.0 copy.75
  376.4 50.8 %all-gather.12.cloned.1.call-done = f32[8,15,4096]{2,1,0:T(8,128)} async-done(((f32[1,15,4096]{2,1,0:T(8,128)}), f32[8,15,4096]{2,1,0:T(8,128)}) %all-gather.12.cloned.1.call-update) | async-done | bytes 1966096 | tf_op jit(solution)/shard_map/all_gather | solution.py:61
  429.6 6.3 all-reduce
  438.7 7.2 %psum.30 = f32[]{:T(128)} all-reduce(f32[]{:T(128)} %get-tuple-element.13), channel_id=1, replica_groups=mesh['lm'=8,'kf'=4] {'kf'}, use_global_device_ids=true, to_apply=%region_10.12 | all-reduce | flops 1 | bytes 8 | tf_op jit(solution)/shard_map/psum | solution.py:45
  450.8 2.7 copy.78
  453.5 56.6 %gather_fusion.1 = f32[16384,15]{1,0:T(8,128)} fusion(f32[15,8192]{0,1:T(8,128)} %copy.78, s32[16384]{0:T(1024)S(1)} %bitcast_clamp_fusion), kind=kCustom, calls=%fused_computation.1.clone | custom fusion | bytes 2031616 | tf_op jit(solution)/shard_map/jit(_take)/gather | solution.py:56
  510.1 5.4 copy.79
  515.6 3.5 fusion.16
  521.8 4.7 copy.100
  526.4 89.9 %scatter_custom_fusion.2 = f32[15,8192]{0,1:T(8,128)} fusion(s32[16384]{0:T(1024)} %bitcast.85, f32[16384,15]{1,0:T(8,128)} %bitcast.70, f32[]{:T(128)} %constant.1.clone.1), kind=kCustom, calls=%fused_computation.11 | custom fusion | flops 245760 | bytes 492032 | tf_op jit(solution)/shard_map/scatter-add | solution.py:33
  618.5 6.1 collective-permute-start.4
  626.8 3.2 fusion
  630.0 3.0 copy.85
  633.0 51.0 %all-gather.14.cloned.1.call-done = f32[8,15,4096]{2,1,0:T(8,128)} async-done(((f32[1,15,4096]{2,1,0:T(8,128)}), f32[8,15,4096]{2,1,0:T(8,128)}) %all-gather.14.cloned.1.call-update) | async-done | bytes 1966096 | tf_op jit(solution)/shard_map/all_gather | solution.py:61
  686.4 6.3 psum.31
  (97 shorter events, 38.9 us)
Async XLA Ops:
  7.2 181.1 %all-gather.10.cloned.1.call-start = ((), (), s32[]{:S(2)}) async-start(), calls=%async_computation | async-start | bytes 2359296 | tf_op jit(solution)/shard_map/all_gather | solution.py:61
  8.9 3.6 copy-start
  8.9 6.0 copy-start.11
  15.1 9.9 %copy-start.3 = (bf16[128,15,128]{2,0,1:T(8,128)(2,1)S(1)}, bf16[128,15,128]{2,0,1:T(8,128)(2,1)}, u32[]{:S(2)}) copy-start(bf16[128,15,128]{2,0,1:T(8,128)(2,1)} %param.10) | copy-start | bytes 1474564
  25.0 4.8 copy-start.10
  119.7 1.6 slice-start.1
  121.9 3.5 collective-permute-start
  129.2 60.8 %copy-start.5 = (f32[15,4096]{1,0:T(8,128)S(1)}, f32[15,4096]{1,0:T(8,128)}, u32[]{:S(2)}) copy-start(f32[15,4096]{1,0:T(8,128)} %param.15) | copy-start | bytes 737284
  132.2 294.9 %all-gather.12.cloned.1.call-start = ((), (), s32[]{:S(2)}) async-start(), calls=%async_computation.1 | async-start | bytes 2359296 | tf_op jit(solution)/shard_map/all_gather | solution.py:61
  132.3 126.0 %copy-start.8 = (f32[128,128]{1,0:T(8,128)}, f32[128,128]{1,0:T(8,128)S(1)}, u32[]{:S(2)}) copy-start(f32[128,128]{1,0:T(8,128)S(1)} %copy.70) | copy-start | bytes 196612
  190.1 3.4 collective-permute-start.1
  258.2 3.7 copy-start.1
  359.0 1.6 slice-start.2
  361.3 7.3 %collective-permute-start.2 = (f32[15,4096]{1,0:T(8,128)S(1)}, f32[15,4096]{1,0:T(8,128)}, u32[]{:S(2)}, u32[]{:S(2)}) collective-permute-start(f32[15,4096]{1,0:T(8,128)S(1)} %copy.73), channel_id=1, source_target_pairs={{0,1},{1,2},{2,3},{4,5},{5,6},{6,7},{8,9},{9,10},{10,11},{12,13},{... | collective-permute-start | bytes 737288 | tf_op jit(solution)/shard_map/ppermute | solution.py:12
  370.1 58.7 %copy-start.4 = (f32[15,4096]{1,0:T(8,128)S(1)}, f32[15,4096]{1,0:T(8,128)}, u32[]{:S(2)}) copy-start(f32[15,4096]{1,0:T(8,128)} %param.14) | copy-start | bytes 737284
  373.3 64.0 %copy-start.6 = (f32[15,4096]{1,0:T(8,128)S(1)}, f32[15,4096]{1,0:T(8,128)}, u32[]{:S(2)}) copy-start(f32[15,4096]{1,0:T(8,128)} %param.15) | copy-start | bytes 737284
  376.3 307.7 %all-gather.14.cloned.1.call-start = ((), (), s32[]{:S(2)}) async-start(), calls=%async_computation.2 | async-start | bytes 2359296 | tf_op jit(solution)/shard_map/all_gather | solution.py:61
  447.3 3.4 collective-permute-start.3
  510.1 5.5 copy-start.9
  515.4 3.7 copy-start.2
  616.3 1.6 slice-start
  618.5 6.7 collective-permute-start.4
  630.0 64.0 %copy-start.7 = (f32[15,4096]{1,0:T(8,128)S(1)}, f32[15,4096]{1,0:T(8,128)}, u32[]{:S(2)}) copy-start(f32[15,4096]{1,0:T(8,128)} %get-tuple-element.15) | copy-start | bytes 737284
Sparse Core Ops, SparseCore 0:
  132.3 55.9 all-gather.9
  376.4 50.6 all-gather.11
  633.1 50.8 all-gather.13
